TPU v7x, 32 devices: a whole 2x2x4 slice. The times are simulated.
32 devices in a mesh: area: 8 (over z, x), tile: 4 (over y, core).
Axes of the slice: x: 2, y: 2, z: 4, core: 2. Of those that a mesh axis runs over, the one named last changes fastest.
Arguments:
- start_rates: bfloat16 [8, 256, 4096], P('area', None, 'tile'), may hold values from -0.8984375 to 0.8984375
- stim_drive: bfloat16 [8, 256, 4096], P('area', None, 'tile'), may hold values from -6 to 6
- leak_rates: float32 [8, 4096], P('area', 'tile'), may hold values from 0.2 to 0.9
- block_weights: bfloat16 [8, 32, 20, 128, 128], P('area', 'tile'), may hold values from -0.21875 to 0.21875
- near_index: int32 [8, 32, 12], P('area', 'tile'), may hold values from 0 to 9, as said below
- far_index: int32 [8, 32, 8], P('area', 'tile'), may hold values from 0 to 7, as said below
Outputs:
- final_rates: bfloat16 [8, 256, 4096], P('area', None, 'tile')
Inputs may be any that keep to these rules, and one draw needn't show every extreme that they name: `near_index`: an entry names one of the tile's own blocks (1 to 8) or the adjacent edge block of the neighbouring tile (0 the lower, 9 the upper). Slot 0 of every tile's first row block is 0 and slot 1 of every tile's last row block is 9. `far_index`: an entry q names the projecting block (the first block) of the same tile in section q, a section of another area; the areas are the consecutive groups of 3, 2, 2 and 1 eighths of the sections, in that order.
All inputs are finite; a program needn't handle non-finite values.
Results may differ from a plain program's by a relative error of at most 0.005.
Values may be sent and summed in bfloat16 or wider, within the bound.
A program may use at most 64 MiB of HBM per device.

v0:
```python
import jax
import jax.numpy as jnp
from jax import lax
from jax.sharding import PartitionSpec as P

EXPORT = 1
STEPS = 3


def extended(array, sides, width):
    for axis, dim in sides:
        count, length = (lax.axis_size(axis), array.shape[dim])
        up = [(i, (i + 1) % count) for i in range(count - 1)]
        down = [(j, i) for i, j in up]
        last = lax.slice_in_dim(array, length - width, length, axis=dim)
        leading = lax.slice_in_dim(array, 0, width, axis=dim)
        before = lax.ppermute(last, axis, up)
        after = lax.ppermute(leading, axis, down)
        array = jnp.concatenate([before, array, after], axis=dim)
    return array


def select_blocks(flat_rates, slot_index, block_size):
    batch_rows = flat_rates.shape[0]
    blocks = flat_rates.reshape(batch_rows, -1, block_size)
    return jnp.take(blocks, slot_index, axis=1)


def project_blocks(selected, weight_blocks):
    return jnp.einsum("brki,rkio->bro", selected, weight_blocks, preferred_element_type=jnp.float32)


def advance(
    rates_now, padded, export_pool, drive_now, leak_rate, weight_blocks, near_slots, far_slots
):
    block_size = weight_blocks.shape[-1]
    near_selected = select_blocks(padded, near_slots, block_size)
    far_selected = select_blocks(export_pool, far_slots, block_size)
    current = project_blocks(jnp.concatenate((near_selected, far_selected), axis=2), weight_blocks)
    current = current.reshape(rates_now.shape[0], -1) + drive_now
    updated = (1.0 - leak_rate) * rates_now.astype(jnp.float32) + leak_rate * jnp.tanh(current)
    return updated.astype(jnp.bfloat16)


def body(start_rates, stim_drive, leak_rates, block_weights, near_index, far_index):
    rates_now = start_rates[0]
    drive_now = stim_drive[0].astype(jnp.float32)
    leak_rate = leak_rates[0]
    weight_blocks = block_weights[0]
    near_slots = near_index[0]
    far_slots = far_index[0]
    block_size = weight_blocks.shape[-1]
    export_width = EXPORT * block_size
    for step_index in range(STEPS):
        padded = extended(rates_now, (("tile", 1),), block_size)
        export_pool = lax.all_gather(rates_now[:, :export_width], "area", axis=1, tiled=True)
        rates_now = advance(
            rates_now,
            padded,
            export_pool,
            drive_now,
            leak_rate,
            weight_blocks,
            near_slots,
            far_slots,
        )
    return rates_now[None]


def solution(mesh):
    in_specs = (
        P("area", None, "tile"),
        P("area", None, "tile"),
        P("area", "tile"),
        P("area", "tile", None, None, None),
        P("area", "tile", None),
        P("area", "tile", None),
    )
    out_specs = P("area", None, "tile")
    return jax.shard_map(body, mesh=mesh, in_specs=in_specs, out_specs=out_specs, check_vma=False)
```

profile of v0, /device:TPU:1, one launch (start us, length us, event | category | flops | bytes accessed | tf_op | source)
XLA Modules:
  0.0 198.2 jit_solution(1316334638055606450)
XLA Ops:
  0.0 1.2 copy.25
  1.3 1.9 collective-permute-start.1
  3.2 4.5 %collective-permute-start = (bf16[256,128]{0,1:T(8,128)(2,1)S(1)}, bf16[256,128]{0,1:T(8,128)(2,1)S(1)}, u32[]{:S(2)}, u32[]{:S(2)}) collective-permute-start(bf16[256,128]{0,1:T(8,128)(2,1)S(1)} %get-tuple-element.11), channel_id=1, source_target_pairs={{0,1},{1,2},{2,3},{4,5},{5,6},{6,7},{8,9},{9,10},{10,11},{12,13},{... | collective-permute-start | bytes 196616 | tf_op jit(solution)/shard_map/ppermute | solution.py:17
  7.7 0.7 compare_select_fusion.1
  8.4 0.7 compare_and_fusion.1
  9.1 26.1 %all_gather.9 = bf16[256,1024]{0,1:T(8,128)(2,1)S(1)} all-gather(bf16[256,128]{0,1:T(8,128)(2,1)S(1)} %get-tuple-element.12), channel_id=1, replica_groups=mesh['area'=8,'tile'=4] {'area'}, dimensions={1}, use_global_device_ids=true | all-gather | bytes 589824 | tf_op jit(solution)/shard_map/all_gather | solution.py:56
  35.2 0.7 compare_select_fusion
  35.9 0.7 compare_and_fusion
  36.6 0.1 reshape.154
  36.6 0.3 copy.28
  36.9 0.1 reshape.158
  37.0 1.2 copy.30
  38.3 0.7 broadcast_subtract_fusion
  39.0 3.0 %gather_fusion.1 = bf16[64,256,128]{2,1,0:T(8,128)(2,1)} fusion(bf16[256,8,128]{2,0,1:T(8,128)(2,1)S(1)} %copy.28, s32[1024]{0:T(1024)S(1)} %pad_clamp_fusion), kind=kCustom, calls=%fused_computation.1.clone | custom fusion | bytes 8388864 | tf_op jit(solution)/shard_map/jit(_take)/gather | solution.py:26
  42.0 4.6 %select_bitcast_fusion.5 = bf16[256,8,8,128]{3,0,2,1:T(8,128)(2,1)} fusion(bf16[8,8,256,128]{3,2,1,0:T(8,128)(2,1)} %bitcast.93, pred[8,8]{1,0:T(8,128)(4,1)S(1)} %compare_and_fusion), kind=kLoop, calls=%fused_computation.26 | loop fusion | flops 2097152 | bytes 8388672 | tf_op jit(solution)/shard_map/jit(_take)/select_n | solution.py:26
  46.6 0.0 collective-permute-done.1
  46.7 0.0 collective-permute-done
  46.7 0.3 copy.27
  47.0 6.0 %gather_fusion = bf16[96,256,128]{2,1,0:T(8,128)(2,1)} fusion(bf16[256,10,128]{2,0,1:T(8,128)(2,1)S(1)} %copy.27, s32[1024]{0:T(1024)S(1)} %pad_clamp_fusion.1), kind=kCustom, calls=%fused_computation.clone | custom fusion | bytes 12583296 | tf_op jit(solution)/shard_map/jit(_take)/gather | solution.py:26
  53.0 3.4 %select_bitcast_fusion.2 = bf16[256,8,12,128]{3,0,2,1:T(8,128)(2,1)S(1)} fusion(bf16[8,12,256,128]{3,2,1,0:T(8,128)(2,1)} %bitcast.90, pred[8,12]{1,0:T(8,128)(4,1)S(1)} %compare_and_fusion.1), kind=kLoop, calls=%fused_computation.20 | loop fusion | flops 3145728 | bytes 12583008 | tf_op jit(solution)/shard_map/jit(_take)/select_n | solution.py:26
  56.4 0.0 copy-start.4
  56.5 6.1 %fusion = f32[8,256,128,1]{1,2,3,0:T(8,128)S(1)} fusion(bf16[256,8,8,128]{3,0,2,1:T(8,128)(2,1)} %select_bitcast_fusion.5, bf16[256,8,12,128]{3,0,2,1:T(8,128)(2,1)S(1)} %select_bitcast_fusion.2, bf16[1,8,20,128,128]{4,3,2,1,0:T(8,128)(2,1)} %param.13), kind=kOutput, calls=%fused_computation.6 | convolution fusion | flops 1347420160 | bytes 16777216 | tf_op jit(solution)/shard_map/brki,rkio->bro/dot_general | solution.py:30
  62.6 0.0 copy-done.4
  62.6 0.3 fusion.20
  63.0 6.9 %collective-permute-start.3 = (bf16[256,128]{0,1:T(8,128)(2,1)S(1)}, bf16[256,128]{0,1:T(8,128)(2,1)S(1)}, u32[]{:S(2)}, u32[]{:S(2)}) collective-permute-start(bf16[256,128]{0,1:T(8,128)(2,1)S(1)} %get-tuple-element.10), channel_id=1, source_target_pairs={{1,0},{2,1},{3,2},{5,4},{6,5},{7,6},{9,8},{10,9},{11,10},{13,12},{... | collective-permute-start | bytes 196616 | tf_op jit(solution)/shard_map/ppermute | solution.py:18
  69.9 28.0 %all_gather.10 = bf16[256,1024]{0,1:T(8,128)(2,1)} all-gather(bf16[256,128]{0,1:T(8,128)(2,1)S(1)} %get-tuple-element.10), channel_id=1, replica_groups=mesh['area'=8,'tile'=4] {'area'}, dimensions={1}, use_global_device_ids=true | all-gather | bytes 589824 | tf_op jit(solution)/shard_map/all_gather | solution.py:56
  97.9 8.5 %collective-permute-start.2 = (bf16[256,128]{0,1:T(8,128)(2,1)S(1)}, bf16[256,128]{0,1:T(8,128)(2,1)S(1)}, u32[]{:S(2)}, u32[]{:S(2)}) collective-permute-start(bf16[256,128]{0,1:T(8,128)(2,1)S(1)} %get-tuple-element.9), channel_id=1, source_target_pairs={{0,1},{1,2},{2,3},{4,5},{5,6},{6,7},{8,9},{9,10},{10,11},{12,13},{... | collective-permute-start | bytes 196616 | tf_op jit(solution)/shard_map/ppermute | solution.py:17
  106.4 1.3 copy.32
  107.8 3.0 %gather_fusion.3 = bf16[64,256,128]{2,1,0:T(8,128)(2,1)} fusion(bf16[256,8,128]{2,0,1:T(8,128)(2,1)S(1)} %copy.32, s32[1024]{0:T(1024)S(1)} %pad_clamp_fusion), kind=kCustom, calls=%fused_computation.4.clone | custom fusion | bytes 8388864 | tf_op jit(solution)/shard_map/jit(_take)/gather | solution.py:26
  110.8 4.6 %select_bitcast_fusion.4 = bf16[256,8,8,128]{3,0,2,1:T(8,128)(2,1)} fusion(bf16[8,8,256,128]{3,2,1,0:T(8,128)(2,1)} %bitcast.94, pred[8,8]{1,0:T(8,128)(4,1)S(1)} %compare_and_fusion), kind=kLoop, calls=%fused_computation.25 | loop fusion | flops 2097152 | bytes 8388672 | tf_op jit(solution)/shard_map/jit(_take)/select_n | solution.py:26
  115.4 0.0 collective-permute-done.3
  115.4 0.0 collective-permute-done.2
  115.4 0.9 pad_maximum_fusion.1
  116.3 1.4 copy.31
  117.8 6.0 %gather_fusion.2 = bf16[96,256,128]{2,1,0:T(8,128)(2,1)} fusion(bf16[256,10,128]{2,0,1:T(8,128)(2,1)S(1)} %copy.31, s32[1024]{0:T(1024)S(1)} %pad_clamp_fusion.1), kind=kCustom, calls=%fused_computation.2.clone | custom fusion | bytes 12583296 | tf_op jit(solution)/shard_map/jit(_take)/gather | solution.py:26
  123.7 3.4 %select_bitcast_fusion.1 = bf16[256,8,12,128]{3,0,2,1:T(8,128)(2,1)S(1)} fusion(bf16[8,12,256,128]{3,2,1,0:T(8,128)(2,1)} %bitcast.91, pred[8,12]{1,0:T(8,128)(4,1)S(1)} %compare_and_fusion.1), kind=kLoop, calls=%fused_computation.19 | loop fusion | flops 3145728 | bytes 12583008 | tf_op jit(solution)/shard_map/jit(_take)/select_n | solution.py:26
  127.2 6.1 %fusion.4 = f32[8,256,128,1]{1,2,3,0:T(8,128)S(1)} fusion(bf16[256,8,8,128]{3,0,2,1:T(8,128)(2,1)} %select_bitcast_fusion.4, bf16[256,8,12,128]{3,0,2,1:T(8,128)(2,1)S(1)} %select_bitcast_fusion.1, bf16[1,8,20,128,128]{4,3,2,1,0:T(8,128)(2,1)} %param.13), kind=kOutput, calls=%fused_computation.10 | convolution fusion | flops 1347420160 | bytes 16777216 | tf_op jit(solution)/shard_map/brki,rkio->bro/dot_general | solution.py:30
  133.3 0.0 copy-start
  133.3 0.3 fusion.24
  133.6 0.0 copy-start.2
  133.7 1.9 collective-permute-start.5
  135.6 25.4 %all_gather.11 = bf16[256,1024]{0,1:T(8,128)(2,1)S(1)} all-gather(bf16[256,128]{0,1:T(8,128)(2,1)S(1)} %get-tuple-element.8), channel_id=1, replica_groups=mesh['area'=8,'tile'=4] {'area'}, dimensions={1}, use_global_device_ids=true | all-gather | bytes 589824 | tf_op jit(solution)/shard_map/all_gather | solution.py:56
  161.0 9.6 %collective-permute-start.4 = (bf16[256,128]{0,1:T(8,128)(2,1)S(1)}, bf16[256,128]{0,1:T(8,128)(2,1)S(1)}, u32[]{:S(2)}, u32[]{:S(2)}) collective-permute-start(bf16[256,128]{0,1:T(8,128)(2,1)S(1)} %get-tuple-element.6), channel_id=1, source_target_pairs={{0,1},{1,2},{2,3},{4,5},{5,6},{6,7},{8,9},{9,10},{10,11},{12,13},{... | collective-permute-start | bytes 196616 | tf_op jit(solution)/shard_map/ppermute | solution.py:17
  170.5 0.0 copy-done
  170.6 0.0 copy-done.2
  170.6 0.3 copy.35
  170.8 3.0 %gather_fusion.5 = bf16[64,256,128]{2,1,0:T(8,128)(2,1)} fusion(bf16[256,8,128]{2,0,1:T(8,128)(2,1)S(1)} %copy.35, s32[1024]{0:T(1024)S(1)} %pad_clamp_fusion), kind=kCustom, calls=%fused_computation.5.clone | custom fusion | bytes 8388864 | tf_op jit(solution)/shard_map/jit(_take)/gather | solution.py:26
  173.9 0.0 copy-start.3
  173.9 4.7 %select_bitcast_fusion.3 = bf16[256,8,8,128]{3,0,2,1:T(8,128)(2,1)} fusion(bf16[8,8,256,128]{3,2,1,0:T(8,128)(2,1)} %bitcast.92, pred[8,8]{1,0:T(8,128)(4,1)S(1)} %compare_and_fusion), kind=kLoop, calls=%fused_computation.24 | loop fusion | flops 2097152 | bytes 8388672 | tf_op jit(solution)/shard_map/jit(_take)/select_n | solution.py:26
  178.6 0.0 collective-permute-done.4
  178.6 0.0 collective-permute-done.5
  178.6 0.0 copy-done.3
  178.6 0.9 pad_maximum_fusion.2
  179.5 1.4 copy.34
  180.9 6.0 %gather_fusion.4 = bf16[96,256,128]{2,1,0:T(8,128)(2,1)} fusion(bf16[256,10,128]{2,0,1:T(8,128)(2,1)S(1)} %copy.34, s32[1024]{0:T(1024)S(1)} %pad_clamp_fusion.1), kind=kCustom, calls=%fused_computation.3.clone | custom fusion | bytes 12583296 | tf_op jit(solution)/shard_map/jit(_take)/gather | solution.py:26
  186.9 3.4 %select_bitcast_fusion = bf16[256,8,12,128]{3,0,2,1:T(8,128)(2,1)S(1)} fusion(bf16[8,12,256,128]{3,2,1,0:T(8,128)(2,1)} %bitcast.89, pred[8,12]{1,0:T(8,128)(4,1)S(1)} %compare_and_fusion.1), kind=kLoop, calls=%fused_computation.18 | loop fusion | flops 3145728 | bytes 12583008 | tf_op jit(solution)/shard_map/jit(_take)/select_n | solution.py:26
  190.3 0.0 copy-start.1
  190.3 6.2 %fusion.8 = f32[8,256,128,1]{1,2,3,0:T(8,128)S(1)} fusion(bf16[256,8,8,128]{3,0,2,1:T(8,128)(2,1)} %select_bitcast_fusion.3, bf16[256,8,12,128]{3,0,2,1:T(8,128)(2,1)S(1)} %select_bitcast_fusion, bf16[1,8,20,128,128]{4,3,2,1,0:T(8,128)(2,1)} %param.13), kind=kOutput, calls=%fused_computation.14 | convolution fusion | flops 1347420160 | bytes 16777216 | tf_op jit(solution)/shard_map/brki,rkio->bro/dot_general | solution.py:30
  196.5 0.0 copy-done.1
  196.5 0.6 fusion.36
  197.2 1.0 copy.37
  (6 shorter events, 0.1 us)
Async XLA Ops:
  1.3 45.4 %collective-permute-start.1 = (bf16[256,128]{0,1:T(8,128)(2,1)S(1)}, bf16[256,128]{0,1:T(8,128)(2,1)S(1)}, u32[]{:S(2)}, u32[]{:S(2)}) collective-permute-start(bf16[256,128]{0,1:T(8,128)(2,1)S(1)} %get-tuple-element.12), channel_id=1, source_target_pairs={{1,0},{2,1},{3,2},{5,4},{6,5},{7,6},{9,8},{10,9},{11,10},{13,12},{... | collective-permute-start | bytes 196616 | tf_op jit(solution)/shard_map/ppermute | solution.py:18
  3.2 43.5 %collective-permute-start = (bf16[256,128]{0,1:T(8,128)(2,1)S(1)}, bf16[256,128]{0,1:T(8,128)(2,1)S(1)}, u32[]{:S(2)}, u32[]{:S(2)}) collective-permute-start(bf16[256,128]{0,1:T(8,128)(2,1)S(1)} %get-tuple-element.11), channel_id=1, source_target_pairs={{0,1},{1,2},{2,3},{4,5},{5,6},{6,7},{8,9},{9,10},{10,11},{12,13},{... | collective-permute-start | bytes 196616 | tf_op jit(solution)/shard_map/ppermute | solution.py:17
  56.4 6.2 %copy-start.4 = (f32[1,1024]{1,0:T(1,128)S(1)}, f32[1,1024]{1,0:T(1,128)}, u32[]{:S(2)}) copy-start(f32[1,1024]{1,0:T(1,128)} %param.12) | copy-start | bytes 12292
  63.0 52.5 %collective-permute-start.3 = (bf16[256,128]{0,1:T(8,128)(2,1)S(1)}, bf16[256,128]{0,1:T(8,128)(2,1)S(1)}, u32[]{:S(2)}, u32[]{:S(2)}) collective-permute-start(bf16[256,128]{0,1:T(8,128)(2,1)S(1)} %get-tuple-element.10), channel_id=1, source_target_pairs={{1,0},{2,1},{3,2},{5,4},{6,5},{7,6},{9,8},{10,9},{11,10},{13,12},{... | collective-permute-start | bytes 196616 | tf_op jit(solution)/shard_map/ppermute | solution.py:18
  97.9 17.6 %collective-permute-start.2 = (bf16[256,128]{0,1:T(8,128)(2,1)S(1)}, bf16[256,128]{0,1:T(8,128)(2,1)S(1)}, u32[]{:S(2)}, u32[]{:S(2)}) collective-permute-start(bf16[256,128]{0,1:T(8,128)(2,1)S(1)} %get-tuple-element.9), channel_id=1, source_target_pairs={{0,1},{1,2},{2,3},{4,5},{5,6},{6,7},{8,9},{9,10},{10,11},{12,13},{... | collective-permute-start | bytes 196616 | tf_op jit(solution)/shard_map/ppermute | solution.py:17
  133.3 37.3 %copy-start = (f32[8,256,128,1]{1,2,3,0:T(8,128)}, f32[8,256,128,1]{1,2,3,0:T(8,128)S(1)}, u32[]{:S(2)}) copy-start(f32[8,256,128,1]{1,2,3,0:T(8,128)S(1)} %fusion.4) | copy-start | bytes 3145732
  133.6 36.9 %copy-start.2 = (bf16[256,1024]{0,1:T(8,128)(2,1)}, bf16[256,1024]{0,1:T(8,128)(2,1)S(1)}, u32[]{:S(2)}) copy-start(bf16[256,1024]{0,1:T(8,128)(2,1)S(1)} %fusion.24) | copy-start | bytes 1572868
  133.7 44.9 %collective-permute-start.5 = (bf16[256,128]{0,1:T(8,128)(2,1)S(1)}, bf16[256,128]{0,1:T(8,128)(2,1)S(1)}, u32[]{:S(2)}, u32[]{:S(2)}) collective-permute-start(bf16[256,128]{0,1:T(8,128)(2,1)S(1)} %get-tuple-element.8), channel_id=1, source_target_pairs={{1,0},{2,1},{3,2},{5,4},{6,5},{7,6},{9,8},{10,9},{11,10},{13,12},{... | collective-permute-start | bytes 196616 | tf_op jit(solution)/shard_map/ppermute | solution.py:18
  161.0 17.6 %collective-permute-start.4 = (bf16[256,128]{0,1:T(8,128)(2,1)S(1)}, bf16[256,128]{0,1:T(8,128)(2,1)S(1)}, u32[]{:S(2)}, u32[]{:S(2)}) collective-permute-start(bf16[256,128]{0,1:T(8,128)(2,1)S(1)} %get-tuple-element.6), channel_id=1, source_target_pairs={{0,1},{1,2},{2,3},{4,5},{5,6},{6,7},{8,9},{9,10},{10,11},{12,13},{... | collective-permute-start | bytes 196616 | tf_op jit(solution)/shard_map/ppermute | solution.py:17
  173.9 4.7 %copy-start.3 = (bf16[256,1024]{0,1:T(8,128)(2,1)S(1)}, bf16[256,1024]{0,1:T(8,128)(2,1)}, u32[]{:S(2)}) copy-start(bf16[256,1024]{0,1:T(8,128)(2,1)} %copy-done.2) | copy-start | bytes 1572868
  190.3 6.2 %copy-start.1 = (f32[8,256,128,1]{1,2,3,0:T(8,128)S(1)}, f32[8,256,128,1]{1,2,3,0:T(8,128)}, u32[]{:S(2)}) copy-start(f32[8,256,128,1]{1,2,3,0:T(8,128)} %copy-done) | copy-start | bytes 3145732
where the time goes:
time: 199 us; the launch traced here: 198 us
  blocking collectives  79.5 us (40%)
  local copies, waits for them, and re-layouts  35.7 us (18%)
  starting transfers between devices  33.4 us (17%)
  other arithmetic  30.8 us (15%)
  matrix products  18.5 us (9%)
    all_gather x3, blocking collectives, body(): lax.all_gather(rates_now[:, :export_width], 'area', axis=1, tiled=True)  79.5 us
    gather x6, local copies, waits for them, and re-layouts, select_blocks(): return jnp.take(blocks, slot_index, axis=1)  27 us
    select_n x8, other arithmetic, select_blocks(): return jnp.take(blocks, slot_index, axis=1)  25.6 us
    ppermute x3, starting transfers between devices, extended(): before = lax.ppermute(last, axis, up)  22.6 us
    dot_general x3, matrix products, project_blocks(): jnp.einsum('brki,rkio->bro', selected, weight_blocks, preferred_element_t...  18.5 us
    ppermute x3, starting transfers between devices, extended(): after = lax.ppermute(leading, axis, down)  10.7 us
    reshape x6, local copies, waits for them, and re-layouts, select_blocks(): blocks = flat_rates.reshape(batch_rows, -1, block_size)  4.99 us
  transfers between devices with their start and end apart: 6, of which 0 were waited for; matrix products, arithmetic and copies ran while one was open for 15% of the time, Pallas kernels for 0%

commit v1 on v0

v1 whole, which is shorter than its diff:
```python
import functools

import jax
import jax.numpy as jnp
from jax import lax
from jax.experimental import pallas as pl
from jax.experimental.pallas import tpu as pltpu
from jax.sharding import PartitionSpec as P

STEPS = 3
CHUNKS = 2
MESH = pl.DeviceIdType.MESH


def group_of(section, n_area):
    unit = n_area // 8
    return (
        (section >= 3 * unit).astype(jnp.int32)
        + (section >= 5 * unit).astype(jnp.int32)
        + (section >= 7 * unit).astype(jnp.int32)
    )


def kernel(sizes, near_idx, far_idx, rates_hbm, drive_hbm, leak_ref, w_hbm, out_hbm, *scratch):
    n_area, n_tile, batch, rows, k_near, k_far, blk = sizes
    n_col = n_area // 2
    part = batch // CHUNKS
    nears = scratch[:STEPS]
    final = scratch[STEPS]
    scratch = scratch[STEPS + 1 :]
    fars = [scratch[t * CHUNKS : (t + 1) * CHUNKS] for t in range(STEPS)]
    (
        drive, weights, acc,
        load_sem, drive_sem, w_sem, out_sem,
        far_recv, col_send, own_send, relay_send, edge_send, edge_recv,
    ) = scratch[STEPS * CHUNKS :]

    area = lax.axis_index("area")
    tile = lax.axis_index("tile")
    side = lax.rem(area, 2)
    level = area // 2
    partner = area + 1 - 2 * side

    def needs(section, source):
        return group_of(section, n_area) != group_of(source, n_area)

    def column_needs(section, source):
        mate = section + 1 - 2 * lax.rem(section, 2)
        return jnp.logical_or(needs(section, source), needs(mate, source))

    def offsets(far_first):
        steps = range(n_col - 1, 0, -1) if far_first else range(1, n_col)
        return [s * d for d in steps for s in (1, -1)]

    def inside(offset):
        return jnp.logical_and(level + offset >= 0, level + offset < n_col)

    def member(offset):
        return area + 2 * offset

    def span(c):
        return pl.ds(c * part, part)

    def load(r):
        return pltpu.make_async_copy(
            rates_hbm.at[:, pl.ds(r * blk, blk)], nears[0].at[r + 1], load_sem.at[r]
        )

    def load_drive(r):
        return pltpu.make_async_copy(
            drive_hbm.at[:, pl.ds(r * blk, blk)], drive.at[r], drive_sem.at[r]
        )

    def load_weights(r):
        return pltpu.make_async_copy(w_hbm.at[r], weights.at[r], w_sem.at[r])

    order = [0, rows - 1] + list(range(1, rows - 1))
    for r in order:
        load(r).start()
    for r in range(rows):
        load_weights(r).start()
        load_drive(r).start()

    barrier = pltpu.get_barrier_semaphore()
    for offset in offsets(True):
        @pl.when(inside(offset))
        def _(offset=offset):
            pl.semaphore_signal(
                barrier, inc=1, device_id=(member(offset), tile), device_id_type=MESH
            )
    pl.semaphore_signal(barrier, inc=1, device_id=(partner, tile), device_id_type=MESH)
    has_low = tile > 0
    has_high = tile < n_tile - 1

    @pl.when(has_low)
    def _():
        pl.semaphore_signal(barrier, inc=1, device_id=(area, tile - 1), device_id_type=MESH)

    @pl.when(has_high)
    def _():
        pl.semaphore_signal(barrier, inc=1, device_id=(area, tile + 1), device_id_type=MESH)

    for t in range(STEPS):
        @pl.when(jnp.logical_not(has_low))
        def _(t=t):
            nears[t][0] = jnp.zeros((batch, blk), jnp.bfloat16)

        @pl.when(jnp.logical_not(has_high))
        def _(t=t):
            nears[t][rows + 1] = jnp.zeros((batch, blk), jnp.bfloat16)

    pl.semaphore_wait(
        barrier, n_col + has_low.astype(jnp.int32) + has_high.astype(jnp.int32)
    )

    def column_copy(t, c, offset):
        return pltpu.make_async_remote_copy(
            src_ref=nears[t].at[1, span(c)],
            dst_ref=fars[t][c].at[area],
            send_sem=col_send.at[t, c, offset + n_col - 1],
            recv_sem=far_recv.at[t, c, area],
            device_id=(member(offset), tile),
            device_id_type=MESH,
        )

    def own_copy(t, c):
        return pltpu.make_async_remote_copy(
            src_ref=nears[t].at[1, span(c)],
            dst_ref=fars[t][c].at[area],
            send_sem=own_send.at[t, c],
            recv_sem=far_recv.at[t, c, area],
            device_id=(partner, tile),
            device_id_type=MESH,
        )

    def relay_copy(t, c, offset):
        source = member(offset)
        return pltpu.make_async_remote_copy(
            src_ref=fars[t][c].at[source],
            dst_ref=fars[t][c].at[source],
            send_sem=relay_send.at[t, c, offset + n_col - 1],
            recv_sem=far_recv.at[t, c, source],
            device_id=(partner, tile),
            device_id_type=MESH,
        )

    def arrival(t, c, source):
        return pltpu.make_async_remote_copy(
            src_ref=nears[t].at[1, span(c)],
            dst_ref=fars[t][c].at[source],
            send_sem=own_send.at[t, c],
            recv_sem=far_recv.at[t, c, source],
            device_id=(partner, tile),
            device_id_type=MESH,
        )

    def low_copy(t):
        return pltpu.make_async_remote_copy(
            src_ref=nears[t].at[1],
            dst_ref=nears[t].at[rows + 1],
            send_sem=edge_send.at[t, 0],
            recv_sem=edge_recv.at[t, 1],
            device_id=(area, tile - 1),
            device_id_type=MESH,
        )

    def high_copy(t):
        return pltpu.make_async_remote_copy(
            src_ref=nears[t].at[rows],
            dst_ref=nears[t].at[0],
            send_sem=edge_send.at[t, 1],
            recv_sem=edge_recv.at[t, 0],
            device_id=(area, tile + 1),
            device_id_type=MESH,
        )

    def send_export(t, c):
        for offset in offsets(True):
            @pl.when(inside(offset))
            def _(offset=offset):
                @pl.when(column_needs(member(offset), area))
                def _():
                    column_copy(t, c, offset).start()

        @pl.when(needs(partner, area))
        def _():
            own_copy(t, c).start()

    def send_low(t):
        @pl.when(has_low)
        def _():
            low_copy(t).start()

    def send_high(t):
        @pl.when(has_high)
        def _():
            high_copy(t).start()

    def wait_edges(t):
        @pl.when(has_high)
        def _():
            low_copy(t).wait_recv()

        @pl.when(has_low)
        def _():
            high_copy(t).wait_recv()

    def relay(t, c):
        for offset in offsets(False):
            @pl.when(inside(offset))
            def _(offset=offset):
                @pl.when(column_needs(area, member(offset)))
                def _():
                    arrival(t, c, member(offset)).wait_recv()

                @pl.when(needs(partner, member(offset)))
                def _():
                    relay_copy(t, c, offset).start()

    def wait_partner(t, c):
        @pl.when(needs(area, partner))
        def _():
            arrival(t, c, partner).wait_recv()

        for offset in offsets(False):
            @pl.when(inside(offset))
            def _(offset=offset):
                source = partner + 2 * offset

                @pl.when(needs(area, source))
                def _():
                    arrival(t, c, source).wait_recv()

    def chain(pieces, w_of):
        total = None
        for k in range(0, len(pieces), 2):
            pair = jnp.concatenate([p() for p in pieces[k : k + 2]], axis=1)
            term = jnp.dot(pair, w_of(k, pair.shape[1]), preferred_element_type=jnp.float32)
            total = term if total is None else total + term
        return total

    def near_row(t, r):
        pieces = [lambda k=k: nears[t][near_idx[r, k]] for k in range(k_near)]
        total = chain(pieces, lambda k, n: weights[r, pl.ds(k * blk, n), :])
        acc[r] = total + drive[r].astype(jnp.float32)

    def blend(t, r, current, rates):
        leak = leak_ref[r]
        return ((1.0 - leak) * rates.astype(jnp.float32) + leak * jnp.tanh(current)).astype(
            jnp.bfloat16
        )

    def far_row(t, r, chunks):
        if len(chunks) == 1:
            rows_of = span(chunks[0])
        else:
            rows_of = slice(None)
        pieces = [
            lambda k=k: jnp.concatenate([fars[t][c][far_idx[r, k]] for c in chunks], axis=0)
            for k in range(k_far)
        ]
        total = chain(pieces, lambda k, n: weights[r, pl.ds((k_near + k) * blk, n), :])
        value = blend(t, r, acc[r, rows_of, :] + total, nears[t][r + 1, rows_of, :])
        if t + 1 < STEPS:
            nears[t + 1][r + 1, rows_of, :] = value
        else:
            final[r, rows_of, :] = value

    def store(r):
        return pltpu.make_async_copy(
            final.at[r], out_hbm.at[:, pl.ds(r * blk, blk)], out_sem.at[r]
        )

    load(0).wait()
    for c in range(CHUNKS):
        send_export(0, c)
    send_low(0)
    load(rows - 1).wait()
    send_high(0)
    for r in range(1, rows - 1):
        load(r).wait()

    everything = list(range(CHUNKS))
    for t in range(STEPS):
        last = t + 1 == STEPS
        wait_edges(t)

        if t == 0:
            for r in range(rows):
                load_drive(r).wait()
                load_weights(r).wait()

        @pl.loop(0, rows)
        def _(r, t=t):
            near_row(t, r)

        for c in everything:
            relay(t, c)
        if not last:
            for c in everything:
                wait_partner(t, c)
                far_row(t, 0, [c])
                send_export(t + 1, c)
            send_low(t + 1)
            far_row(t, rows - 1, everything)
            send_high(t + 1)

            @pl.loop(1, rows - 1)
            def _(r, t=t):
                far_row(t, r, everything)
        else:
            for c in everything:
                wait_partner(t, c)

            @pl.loop(0, rows)
            def _(r, t=t):
                far_row(t, r, everything)
                store(r).start()

    for r in range(rows):
        store(r).wait()
    for t in range(STEPS):
        for c in everything:
            for offset in offsets(True):
                @pl.when(inside(offset))
                def _(t=t, c=c, offset=offset):
                    @pl.when(column_needs(member(offset), area))
                    def _():
                        column_copy(t, c, offset).wait_send()

                    @pl.when(needs(partner, member(offset)))
                    def _():
                        relay_copy(t, c, offset).wait_send()

            @pl.when(needs(partner, area))
            def _(t=t, c=c):
                own_copy(t, c).wait_send()

        @pl.when(has_low)
        def _(t=t):
            low_copy(t).wait_send()

        @pl.when(has_high)
        def _(t=t):
            high_copy(t).wait_send()


def body(n_area, n_tile, start_rates, stim_drive, leak_rates, block_weights, near_index, far_index):
    _, batch, width = start_rates.shape
    _, rows, slots, blk, _ = block_weights.shape
    k_near, k_far = near_index.shape[-1], far_index.shape[-1]
    sizes = (n_area, n_tile, batch, rows, k_near, k_far, blk)
    n_col = n_area // 2
    part = batch // CHUNKS
    any_spec = pl.BlockSpec(memory_space=pl.ANY)
    smem_spec = pl.BlockSpec(memory_space=pltpu.SMEM)
    vmem_spec = pl.BlockSpec(memory_space=pltpu.VMEM)
    dma = pltpu.SemaphoreType.DMA
    scratch = (
        [pltpu.VMEM((rows + 2, batch, blk), jnp.bfloat16) for _ in range(STEPS)]
        + [pltpu.VMEM((rows, batch, blk), jnp.bfloat16)]
        + [pltpu.VMEM((n_area, part, blk), jnp.bfloat16) for _ in range(STEPS * CHUNKS)]
        + [
            pltpu.VMEM((rows, batch, blk), jnp.bfloat16),
            pltpu.VMEM((rows, slots * blk, blk), jnp.bfloat16),
            pltpu.VMEM((rows, batch, blk), jnp.float32),
            dma((rows,)),
            dma((rows,)),
            dma((rows,)),
            dma((rows,)),
            dma((STEPS, CHUNKS, n_area)),
            dma((STEPS, CHUNKS, 2 * n_col - 1)),
            dma((STEPS, CHUNKS)),
            dma((STEPS, CHUNKS, 2 * n_col - 1)),
            dma((STEPS, 2)),
            dma((STEPS, 2)),
        ]
    )
    out = pl.pallas_call(
        functools.partial(kernel, sizes),
        out_shape=jax.ShapeDtypeStruct((batch, width), jnp.bfloat16),
        in_specs=[smem_spec, smem_spec, any_spec, any_spec, vmem_spec, any_spec],
        out_specs=any_spec,
        scratch_shapes=scratch,
        compiler_params=pltpu.CompilerParams(
            collective_id=0, has_side_effects=True, vmem_limit_bytes=56 * 1024 * 1024
        ),
        name="rate_steps",
    )(
        near_index[0],
        far_index[0],
        start_rates[0],
        stim_drive[0],
        leak_rates[0].reshape(rows, 1, blk),
        block_weights[0].reshape(rows, slots * blk, blk),
    )
    return out[None]


def solution(mesh):
    in_specs = (
        P("area", None, "tile"),
        P("area", None, "tile"),
        P("area", "tile"),
        P("area", "tile", None, None, None),
        P("area", "tile", None),
        P("area", "tile", None),
    )
    out_specs = P("area", None, "tile")
    local = functools.partial(body, mesh.shape["area"], mesh.shape["tile"])
    return jax.shard_map(local, mesh=mesh, in_specs=in_specs, out_specs=out_specs, check_vma=False)
```

time: 199 us -> 45.2 us (0.23)
  the two profiles are of different devices: /device:TPU:1 before, /device:TPU:0 now
where the time goes in v1:
time: 45.2 us; the launch traced here: 44.9 us
  Pallas kernels  43 us (95%)
  local copies, waits for them, and re-layouts  1.87 us (4%)
    pallas_call x1, Pallas kernels, body(): pl.pallas_call(functools.partial(kernel, sizes), out_shape=jax.ShapeDtype...  43 us
    unnamed x1, local copies, waits for them, and re-layouts  1.87 us

profile of v1, /device:TPU:0, one launch (start us, length us, event | category | flops | bytes accessed | tf_op | source)
XLA Modules:
  0.0 44.9 jit_solution(9108237103706864651)
XLA Ops:
  0.0 43.0 %rate_steps.1 = bf16[256,1024]{1,0:T(8,128)(2,1)} custom-call(s32[8,12]{1,0:T(8,128)} %bitcast.11, s32[8,8]{1,0:T(8,128)} %bitcast.12, bf16[256,1024]{1,0:T(8,128)(2,1)} %bitcast.9, bf16[256,1024]{1,0:T(8,128)(2,1)} %bitcast.10, f32[8,1,128]{2,1,0:T(1,128)} %bitcast.13, bf16[8,2560,128]{2,1,0:T(8,128)(2,1)} %bitcast.7), custom_call_target="tpu_custom_call" | custom-call | tf_op jit(solution)/shard_map/rate_steps/pallas_call | solution.py:379
  43.0 1.9 %copy.8 = bf16[1,256,1024]{2,1,0:T(8,128)(2,1)} copy(bf16[1,256,1024]{2,1,0:T(8,128)(2,1)} %bitcast.8) | data formatting | bytes 1048576

commit v2 on v1

--- a/solution.py
+++ b/solution.py
@@ -9,6 +9,8 @@
 
 STEPS = 3
 CHUNKS = 2
+LEAD = 1
+UNROLL = 2
 MESH = pl.DeviceIdType.MESH
 
 
@@ -21,17 +23,16 @@
     )
 
 
-def kernel(sizes, near_idx, far_idx, rates_hbm, drive_hbm, leak_ref, w_hbm, out_hbm, *scratch):
+def kernel(sizes, near_idx, far_idx, rates_hbm, drive_hbm, leak_ref, w_hbm, out_ref, *scratch):
     n_area, n_tile, batch, rows, k_near, k_far, blk = sizes
     n_col = n_area // 2
     part = batch // CHUNKS
     nears = scratch[:STEPS]
-    final = scratch[STEPS]
-    scratch = scratch[STEPS + 1 :]
+    scratch = scratch[STEPS:]
     fars = [scratch[t * CHUNKS : (t + 1) * CHUNKS] for t in range(STEPS)]
     (
         drive, weights, acc,
-        load_sem, drive_sem, w_sem, out_sem,
+        load_sem, drive_sem, w_sem,
         far_recv, col_send, own_send, relay_send, edge_send, edge_recv,
     ) = scratch[STEPS * CHUNKS :]
 
@@ -264,12 +265,7 @@
         if t + 1 < STEPS:
             nears[t + 1][r + 1, rows_of, :] = value
         else:
-            final[r, rows_of, :] = value
-
-    def store(r):
-        return pltpu.make_async_copy(
-            final.at[r], out_hbm.at[:, pl.ds(r * blk, blk)], out_sem.at[r]
-        )
+            out_ref[rows_of, pl.ds(pl.multiple_of(r * blk, blk), blk)] = value
 
     load(0).wait()
     for c in range(CHUNKS):
@@ -281,44 +277,49 @@
         load(r).wait()
 
     everything = list(range(CHUNKS))
+
+    def near_rows(t, first, count):
+        @pl.loop(first, first + count, unroll=UNROLL)
+        def _(r):
+            near_row(t, r)
+
+    def near_part(t):
+        wait_edges(t)
+        share = rows // 2
+        relay(t, 0)
+        near_rows(t, 0, share)
+        for c in range(1, 1 + LEAD):
+            relay(t, c)
+        near_rows(t, share, rows - share)
+
+    for r in range(rows):
+        load_weights(r).wait()
+        load_drive(r).wait()
+    near_part(0)
     for t in range(STEPS):
         last = t + 1 == STEPS
-        wait_edges(t)
-
-        if t == 0:
-            for r in range(rows):
-                load_drive(r).wait()
-                load_weights(r).wait()
-
-        @pl.loop(0, rows)
-        def _(r, t=t):
-            near_row(t, r)
-
         for c in everything:
-            relay(t, c)
-        if not last:
-            for c in everything:
-                wait_partner(t, c)
+            wait_partner(t, c)
+            if not last:
                 far_row(t, 0, [c])
                 send_export(t + 1, c)
+            if c + 1 + LEAD < CHUNKS:
+                relay(t, c + 1 + LEAD)
+        if not last:
             send_low(t + 1)
             far_row(t, rows - 1, everything)
             send_high(t + 1)
 
-            @pl.loop(1, rows - 1)
+            @pl.loop(1, rows - 1, unroll=UNROLL)
             def _(r, t=t):
                 far_row(t, r, everything)
+
+            near_part(t + 1)
         else:
-            for c in everything:
-                wait_partner(t, c)
-
-            @pl.loop(0, rows)
+            @pl.loop(0, rows, unroll=UNROLL)
             def _(r, t=t):
                 far_row(t, r, everything)
-                store(r).start()
-
-    for r in range(rows):
-        store(r).wait()
+
     for t in range(STEPS):
         for c in everything:
             for offset in offsets(True):
@@ -328,6 +329,8 @@
                     def _():
                         column_copy(t, c, offset).wait_send()
 
+                @pl.when(inside(offset))
+                def _(t=t, c=c, offset=offset):
                     @pl.when(needs(partner, member(offset)))
                     def _():
                         relay_copy(t, c, offset).wait_send()
@@ -358,13 +361,11 @@
     dma = pltpu.SemaphoreType.DMA
     scratch = (
         [pltpu.VMEM((rows + 2, batch, blk), jnp.bfloat16) for _ in range(STEPS)]
-        + [pltpu.VMEM((rows, batch, blk), jnp.bfloat16)]
         + [pltpu.VMEM((n_area, part, blk), jnp.bfloat16) for _ in range(STEPS * CHUNKS)]
         + [
             pltpu.VMEM((rows, batch, blk), jnp.bfloat16),
             pltpu.VMEM((rows, slots * blk, blk), jnp.bfloat16),
             pltpu.VMEM((rows, batch, blk), jnp.float32),
-            dma((rows,)),
             dma((rows,)),
             dma((rows,)),
             dma((rows,)),
@@ -378,9 +379,9 @@
     )
     out = pl.pallas_call(
         functools.partial(kernel, sizes),
-        out_shape=jax.ShapeDtypeStruct((batch, width), jnp.bfloat16),
+        out_shape=pltpu.MemorySpace.VMEM((batch, width), jnp.bfloat16),
         in_specs=[smem_spec, smem_spec, any_spec, any_spec, vmem_spec, any_spec],
-        out_specs=any_spec,
+        out_specs=vmem_spec,
         scratch_shapes=scratch,
         compiler_params=pltpu.CompilerParams(
             collective_id=0, has_side_effects=True, vmem_limit_bytes=56 * 1024 * 1024

time: 45.2 us -> 39.4 us (0.87)
  Pallas kernels: 43 us -> 38.4 us
  local copies, waits for them, and re-layouts: 1.87 us -> 0.8 us
    pallas_call x1, Pallas kernels: 43 us -> 38.4 us  [body(): pl.pallas_call(functools.partial(kernel, sizes), out_shape=pltpu.MemorySp...]
    unnamed x1, local copies, waits for them, and re-layouts: 1.87 us -> 0.8 us
where the time goes in v2:
time: 39.4 us; the launch traced here: 39.2 us
  Pallas kernels  38.4 us (97%)
  local copies, waits for them, and re-layouts  0.8 us (2%)
    pallas_call x1, Pallas kernels, body(): pl.pallas_call(functools.partial(kernel, sizes), out_shape=pltpu.MemorySp...  38.4 us
    unnamed x1, local copies, waits for them, and re-layouts  0.8 us

profile of v2, /device:TPU:0, one launch (start us, length us, event | category | flops | bytes accessed | tf_op | source)
XLA Modules:
  0.0 39.2 jit_solution(7456251433450202583)
XLA Ops:
  0.0 38.4 %rate_steps.1 = bf16[256,1024]{1,0:T(8,128)(2,1)S(1)} custom-call(s32[8,12]{1,0:T(8,128)} %bitcast.11, s32[8,8]{1,0:T(8,128)} %bitcast.12, bf16[256,1024]{1,0:T(8,128)(2,1)} %bitcast.9, bf16[256,1024]{1,0:T(8,128)(2,1)} %bitcast.10, f32[8,1,128]{2,1,0:T(1,128)} %bitcast.13, bf16[8,2560,128]{2,1,0:T(8,128)(2,1)} %bitcast.8), custom_call_target="tpu_custom_call" | custom-call | tf_op jit(solution)/shard_map/rate_steps/pallas_call | solution.py:380
  38.4 0.8 %copy.8 = bf16[1,256,1024]{2,1,0:T(8,128)(2,1)} copy(bf16[1,256,1024]{2,1,0:T(8,128)(2,1)S(1)} %bitcast.7) | data formatting | bytes 1048576

commit v3 on v2

--- a/solution.py
+++ b/solution.py
@@ -10,7 +10,7 @@
 STEPS = 3
 CHUNKS = 2
 LEAD = 1
-UNROLL = 2
+UNROLL = 4
 MESH = pl.DeviceIdType.MESH
 
 
@@ -176,7 +176,7 @@
         )
 
     def send_export(t, c):
-        for offset in offsets(True):
+        for offset in offsets(False):
             @pl.when(inside(offset))
             def _(offset=offset):
                 @pl.when(column_needs(member(offset), area))
@@ -300,6 +300,10 @@
         last = t + 1 == STEPS
         for c in everything:
             wait_partner(t, c)
+            if last:
+                @pl.loop(0, rows, unroll=UNROLL)
+                def _(r, t=t, c=c):
+                    far_row(t, r, [c])
             if not last:
                 far_row(t, 0, [c])
                 send_export(t + 1, c)
@@ -310,15 +314,11 @@
             far_row(t, rows - 1, everything)
             send_high(t + 1)
 
-            @pl.loop(1, rows - 1, unroll=UNROLL)
+            @pl.loop(1, rows - 1, unroll=rows - 2)
             def _(r, t=t):
                 far_row(t, r, everything)
 
             near_part(t + 1)
-        else:
-            @pl.loop(0, rows, unroll=UNROLL)
-            def _(r, t=t):
-                far_row(t, r, everything)
 
     for t in range(STEPS):
         for c in everything:

time: 39.4 us -> 37.8 us (0.959)
  Pallas kernels: 38.4 us -> 36.9 us
    pallas_call x1, Pallas kernels: 38.4 us -> 36.9 us  [body(): pl.pallas_call(functools.partial(kernel, sizes), out_shape=pltpu.MemorySp...]
where the time goes in v3:
time: 37.8 us; the launch traced here: 37.7 us
  Pallas kernels  36.9 us (98%)
  local copies, waits for them, and re-layouts  0.8 us (2%)
    pallas_call x1, Pallas kernels, body(): pl.pallas_call(functools.partial(kernel, sizes), out_shape=pltpu.MemorySp...  36.9 us
    unnamed x1, local copies, waits for them, and re-layouts  0.8 us

profile of v3, /device:TPU:0, one launch (start us, length us, event | category | flops | bytes accessed | tf_op | source)
XLA Modules:
  0.0 37.7 jit_solution(14275714432732184523)
XLA Ops:
  0.0 36.9 %rate_steps.1 = bf16[256,1024]{1,0:T(8,128)(2,1)S(1)} custom-call(s32[8,12]{1,0:T(8,128)} %bitcast.11, s32[8,8]{1,0:T(8,128)} %bitcast.12, bf16[256,1024]{1,0:T(8,128)(2,1)} %bitcast.9, bf16[256,1024]{1,0:T(8,128)(2,1)} %bitcast.10, f32[8,1,128]{2,1,0:T(1,128)} %bitcast.13, bf16[8,2560,128]{2,1,0:T(8,128)(2,1)} %bitcast.8), custom_call_target="tpu_custom_call" | custom-call | tf_op jit(solution)/shard_map/rate_steps/pallas_call | solution.py:380
  36.9 0.8 %copy.8 = bf16[1,256,1024]{2,1,0:T(8,128)(2,1)} copy(bf16[1,256,1024]{2,1,0:T(8,128)(2,1)S(1)} %bitcast.7) | data formatting | bytes 1048576
